TPU v7x, 32 devices: a whole 2x2x4 slice. The times are simulated.
32 devices in a mesh: section: 8 (over y, x, core), dp: 4 (over z).
Axes of the slice: x: 2, y: 2, z: 4, core: 2. Of those that a mesh axis runs over, the one named last changes fastest.
Arguments:
- inputs: bfloat16 [4, 8, 128, 4096], P('dp', 'section'), may hold values from -6 to 6
- key_rows: bfloat16 [4, 8, 24, 4096], P('dp', None, None, 'section'), may hold values from -32 to 32
- value_rows: bfloat16 [4, 8, 24, 4096], P('dp', None, None, 'section'), may hold values from -6 to 6
- query_gain: float32 [8, 4096], P('section'), may hold values from 0.1 to 1.9
- cotangent: bfloat16 [4, 8, 128, 4096], P('dp', 'section'), may hold values from -6 to 6
Outputs:
- key_grads: bfloat16 [4, 8, 24, 4096], P('dp', None, None, 'section')
- value_grads: bfloat16 [4, 8, 24, 4096], P('dp', None, None, 'section')
- gain_grads: float32 [8, 4096], P('section')
All inputs are finite; a program needn't handle non-finite values.
Results may differ from a plain program's by a relative error of at most 0.008.
Values may be sent and summed in bfloat16 or wider, within the bound.
A program may use at most 64 MiB of HBM per device.

v0:
```python
import jax
import jax.numpy as jnp
from jax import lax
from jax.sharding import PartitionSpec as P

HEAD = 64
TICKS = 3


def from_behind(x, axis, by):
    length = lax.axis_size(axis)
    return lax.ppermute(x, axis, [(i, (i + by) % length) for i in range(length)])


def product(form, left, right):
    return jnp.einsum(form, left, right, preferred_element_type=jnp.float32)


def attend_forward(states, gain_row, key_block, value_block):
    floats = states.astype(jnp.float32)
    inverse = lax.rsqrt(jnp.mean(floats * floats, axis=-1, keepdims=True) + 1e-06)
    queries = (floats * inverse * gain_row).astype(jnp.bfloat16)
    tok_rows, width = states.shape
    src_rows = key_block.shape[0]
    heads_count = width // HEAD
    query_heads = queries.reshape(tok_rows, heads_count, HEAD)
    key_heads = key_block.reshape(src_rows, heads_count, HEAD)
    value_heads = value_block.reshape(src_rows, heads_count, HEAD)
    scores = product("shd,thd->hst", key_heads, query_heads) * HEAD ** (-0.5)
    highest = jnp.max(scores, axis=1, keepdims=True)
    weights = jnp.exp(scores - highest)
    probs = weights / jnp.sum(weights, axis=1, keepdims=True)
    probs_low = probs.astype(jnp.bfloat16)
    mixed = product("hst,shd->thd", probs_low, value_heads).reshape(tok_rows, width)
    produced = (floats + mixed).astype(jnp.bfloat16)
    return (produced, (inverse, queries, probs, probs_low))


def attend_backward(states, gain_row, key_block, value_block, saved, incoming, needed):
    inverse, queries, probs, probs_low = saved
    tok_rows, width = states.shape
    src_rows = key_block.shape[0]
    heads_count = width // HEAD
    query_heads = queries.reshape(tok_rows, heads_count, HEAD)
    key_heads = key_block.reshape(src_rows, heads_count, HEAD)
    value_heads = value_block.reshape(src_rows, heads_count, HEAD)
    grad_heads = incoming.reshape(tok_rows, heads_count, HEAD)
    dprob = product("shd,thd->hst", value_heads, grad_heads)
    dscore = (
        probs * (dprob - jnp.sum(probs * dprob, axis=1, keepdims=True)) * HEAD ** (-0.5)
    ).astype(jnp.bfloat16)
    value_step = product("hst,thd->shd", probs_low, grad_heads).reshape(src_rows, width)
    key_step = product("hst,thd->shd", dscore, query_heads).reshape(src_rows, width)
    dquery = product("hst,shd->thd", dscore, key_heads).reshape(tok_rows, width)
    unit = states.astype(jnp.float32) * inverse
    gain_step = jnp.sum(dquery * unit, axis=0)
    if needed:
        scaled = gain_row * dquery
        back = incoming.astype(jnp.float32) + inverse * (
            scaled - unit * jnp.mean(scaled * unit, axis=-1, keepdims=True)
        )
        back = back.astype(jnp.bfloat16)
    else:
        back = None
    return (back, key_step, value_step, gain_step)


def on_device(inputs, key_rows, value_rows, query_gain, cotangent):
    arrived = (
        lax.all_to_all(key_rows, "section", split_axis=1, concat_axis=3, tiled=True),
        lax.all_to_all(value_rows, "section", split_axis=1, concat_axis=3, tiled=True),
    )
    local_keys = arrived[0][0, 0]
    local_values = arrived[1][0, 0]
    gain_row = query_gain[0]
    current = inputs[0, 0]
    states = [current]
    for tick_index in range(TICKS):
        if tick_index + 1 < TICKS:
            produced, saved = attend_forward(current, gain_row, local_keys, local_values)
        if tick_index + 1 < TICKS:
            current = from_behind(produced, "section", 1)
            states.append(current)
    key_total = jnp.zeros(local_keys.shape, jnp.float32)
    value_total = jnp.zeros(local_values.shape, jnp.float32)
    gain_total = jnp.zeros(gain_row.shape, jnp.float32)
    carried = cotangent[0, 0]
    for tick_index in range(TICKS - 1, -1, -1):
        incoming = from_behind(carried, "section", -1)
        saved = attend_forward(states[tick_index], gain_row, local_keys, local_values)[1]
        carried, key_step, value_step, gain_step = attend_backward(
            states[tick_index], gain_row, local_keys, local_values, saved, incoming, tick_index > 0
        )
        key_total = key_total + key_step
        value_total = value_total + value_step
        gain_total = gain_total + gain_step
    returned = (
        lax.all_to_all(
            key_total.astype(jnp.bfloat16)[None, None],
            "section",
            split_axis=3,
            concat_axis=1,
            tiled=True,
        ),
        lax.all_to_all(
            value_total.astype(jnp.bfloat16)[None, None],
            "section",
            split_axis=3,
            concat_axis=1,
            tiled=True,
        ),
    )
    gain_summed = lax.psum(gain_total, "dp")
    return (returned[0], returned[1], gain_summed[None])


def solution(mesh):
    return jax.shard_map(
        on_device,
        mesh=mesh,
        in_specs=(
            P("dp", "section", None, None),
            P("dp", None, None, "section"),
            P("dp", None, None, "section"),
            P("section", None),
            P("dp", "section", None, None),
        ),
        out_specs=(
            P("dp", None, None, "section"),
            P("dp", None, None, "section"),
            P("section", None),
        ),
        check_vma=False,
    )
```

profile of v0, /device:TPU:0, one launch (start us, length us, event | category | flops | bytes accessed | tf_op | source)
XLA Modules:
  0.0 241.4 jit_solution(5786657829530134387)
XLA Ops:
  0.6 5.2 %all-to-all-start = ((bf16[1,8,24,512]{3,2,0,1:T(8,128)(2,1)}), bf16[1,8,24,512]{3,2,0,1:T(8,128)(2,1)S(1)}, u32[]{:S(2)}, u32[]{:S(2)}) async-start(bf16[1,8,24,512]{3,2,0,1:T(8,128)(2,1)} %bitcast.148), calls=%async_computation | async-start | bytes 393216 | tf_op jit(solution)/shard_map/all_to_all | solution.py:70
  6.4 1.4 reduce.4
  7.8 1.6 copy.41
  10.0 2.0 all-to-all-done
  12.0 3.4 %all-to-all-start.1 = ((bf16[1,8,24,512]{3,2,0,1:T(8,128)(2,1)}), bf16[1,8,24,512]{3,2,0,1:T(8,128)(2,1)S(1)}, u32[]{:S(2)}, u32[]{:S(2)}) async-start(bf16[1,8,24,512]{3,2,0,1:T(8,128)(2,1)} %bitcast.6), calls=%async_computation.1 | async-start | bytes 393216 | tf_op jit(solution)/shard_map/all_to_all | solution.py:71
  15.5 6.0 %all-to-all-done.1 = bf16[1,8,24,512]{3,2,0,1:T(8,128)(2,1)S(1)} async-done(((bf16[1,8,24,512]{3,2,0,1:T(8,128)(2,1)}), bf16[1,8,24,512]{3,2,0,1:T(8,128)(2,1)S(1)}, u32[]{:S(2)}, u32[]{:S(2)}) %all-to-all-start.1) | async-done | bytes 196640 | tf_op jit(solution)/shard_map/all_to_all | solution.py:71
  22.9 1.8 fusion.114
  24.6 2.0 fusion.90
  26.7 1.2 fusion.31
  27.9 2.3 copy.51
  30.2 2.6 %collective-permute-start.2 = (bf16[128,4096]{0,1:T(8,128)(2,1)}, bf16[128,4096]{0,1:T(8,128)(2,1)}, u32[]{:S(2)}, u32[]{:S(2)}) collective-permute-start(bf16[128,4096]{0,1:T(8,128)(2,1)} %bitcast.18), channel_id=1, source_target_pairs={{0,28},{4,0},{8,4},{12,8},{16,12},{20,16},{24,20},{28,24},{1,29},{... | collective-permute-start | bytes 3145736 | tf_op jit(solution)/shard_map/ppermute | solution.py:12
  32.8 19.4 %collective-permute-done = bf16[128,4096]{0,1:T(8,128)(2,1)S(1)} collective-permute-done((bf16[128,4096]{0,1:T(8,128)(2,1)}, bf16[128,4096]{0,1:T(8,128)(2,1)S(1)}, u32[]{:S(2)}, u32[]{:S(2)}) %collective-permute-start) | collective-permute-done | bytes 1048608 | tf_op jit(solution)/shard_map/ppermute | solution.py:12
  54.9 1.7 fusion.115
  56.5 3.3 %fusion.88 = f32[64,128,64]{1,2,0:T(8,128)} fusion(bf16[24,64,64]{2,1,0:T(8,128)(2,1)S(1)} %reshape_squeeze.5, f32[64,128]{1,0:T(8,128)} %get-tuple-element.15, f32[64,24,128]{2,1,0:T(8,128)} %copy-done.11), kind=kOutput, calls=%fused_computation.108 | convolution fusion | flops 25763864 | bytes 3112960 | tf_op jit(solution)/shard_map/hst,shd->thd/dot_general | solution.py:16
  59.9 1.8 fusion.30
  61.8 2.6 %fusion.86 = f32[64,24,128]{2,1,0:T(8,128)} fusion(bf16[128,64,64]{0,2,1:T(8,128)(2,1)} %bitcast.19, bf16[24,64,64]{2,1,0:T(8,128)(2,1)S(1)} %reshape_squeeze.5), kind=kOutput, calls=%fused_computation.106 | convolution fusion | flops 25165824 | bytes 2031616 | tf_op jit(solution)/shard_map/shd,thd->hst/dot_general | solution.py:16
  64.4 12.5 %collective-permute-done.1 = bf16[128,4096]{0,1:T(8,128)(2,1)S(1)} collective-permute-done((bf16[128,4096]{0,1:T(8,128)(2,1)S(1)}, bf16[128,4096]{0,1:T(8,128)(2,1)S(1)}, u32[]{:S(2)}, u32[]{:S(2)}) %collective-permute-start.1) | collective-permute-done | bytes 1048608 | tf_op jit(solution)/shard_map/ppermute | solution.py:12
  80.5 1.7 fusion.116
  82.2 4.0 %fusion.61 = f32[64,128,64]{1,2,0:T(8,128)} fusion(f32[64,24,128]{2,1,0:T(8,128)} %fusion.86, bf16[24,64,64]{2,1,0:T(8,128)(2,1)} %copy-done.6, f32[64,24,128]{2,1,0:T(8,128)} %get-tuple-element.18, f32[64,128]{1,0:T(8,128)} %get-tuple-element.17), kind=kOutput, calls=%fused_computation.81 | convolution fusion | flops 26550296 | bytes 3899392 | tf_op jit(solution)/shard_map/hst,shd->thd/dot_general | solution.py:16
  86.2 3.3 %fusion.20 = (f32[4096]{0:T(1024)}, f32[128]{0:T(128)S(1)}) fusion(bf16[128,4096]{0,1:T(8,128)(2,1)S(1)} %collective-permute-done.1, f32[64,128,64]{1,2,0:T(8,128)} %fusion.61, f32[128]{0:T(128)} %copy-done.23, f32[4096]{0:T(1024)S(1)} %bitcast.138), kind=kLoop, calls=%fused_computation.25 | loop fusion | flops 3665792 | bytes 3179520 | tf_op jit(solution)/shard_map/reduce_sum | solution.py:56
  89.5 1.9 fusion.19
  91.5 12.3 %collective-permute-done.3 = bf16[128,4096]{0,1:T(8,128)(2,1)S(1)} collective-permute-done((bf16[128,4096]{0,1:T(8,128)(2,1)S(1)}, bf16[128,4096]{0,1:T(8,128)(2,1)S(1)}, u32[]{:S(2)}, u32[]{:S(2)}) %collective-permute-start.3) | collective-permute-done | bytes 1048608 | tf_op jit(solution)/shard_map/ppermute | solution.py:12
  103.8 1.3 convolution_bitcast_fusion.4
  105.1 4.0 %fusion.66 = f32[64,128,64]{1,2,0:T(8,128)} fusion(f32[64,24,128]{2,1,0:T(8,128)} %convolution_bitcast_fusion.4, bf16[24,64,64]{2,1,0:T(8,128)(2,1)} %copy-done.6, f32[64,24,128]{2,1,0:T(8,128)} %get-tuple-element.16, f32[64,128]{1,0:T(8,128)} %get-tuple-element.15), kind=kOutput, calls=%fused_computation.85 | convolution fusion | flops 26550296 | bytes 3899392 | tf_op jit(solution)/shard_map/hst,shd->thd/dot_general | solution.py:16
  109.1 3.3 %fusion.28 = (f32[4096]{0:T(1024)}, f32[128]{0:T(128)S(1)}) fusion(bf16[128,4096]{0,1:T(8,128)(2,1)S(1)} %collective-permute-done, f32[64,128,64]{1,2,0:T(8,128)} %fusion.66, f32[128]{0:T(128)} %copy-done.21, f32[4096]{0:T(1024)S(1)} %bitcast.140), kind=kLoop, calls=%fused_computation.33 | loop fusion | flops 3665792 | bytes 3179520 | tf_op jit(solution)/shard_map/reduce_sum | solution.py:56
  112.3 1.8 fusion.27
  114.2 2.8 %collective-permute-start.4 = (bf16[128,4096]{0,1:T(8,128)(2,1)}, bf16[128,4096]{0,1:T(8,128)(2,1)}, u32[]{:S(2)}, u32[]{:S(2)}) collective-permute-start(bf16[128,4096]{0,1:T(8,128)(2,1)} %fusion.27), channel_id=1, source_target_pairs={{0,28},{4,0},{8,4},{12,8},{16,12},{20,16},{24,20},{28,24},{1,29},{... | collective-permute-start | bytes 3145736 | tf_op jit(solution)/shard_map/ppermute | solution.py:12
  117.0 3.0 %convolution_bitcast_fusion.1 = f32[24,64,64]{2,0,1:T(8,128)} fusion(bf16[128,64,64]{0,2,1:T(8,128)(2,1)S(1)} %bitcast.135, f32[64,128]{1,0:T(8,128)} %get-tuple-element.15, f32[64,24,128]{2,1,0:T(8,128)} %copy-done.11), kind=kOutput, calls=%fused_computation.52 | convolution fusion | flops 25763864 | bytes 2260992 | tf_op jit(solution)/shard_map/hst,thd->shd/dot_general | solution.py:16
  119.9 3.4 %fusion.67 = f32[64,64,24]{1,2,0:T(8,128)} fusion(bf16[128,64,64]{0,2,1:T(8,128)(2,1)S(1)} %bitcast.133, f32[64,24,128]{2,1,0:T(8,128)} %convolution_bitcast_fusion.4, f32[64,24,128]{2,1,0:T(8,128)} %get-tuple-element.16, f32[64,128]{1,0:T(8,128)} %get-tuple-element.15), kind=kOutput, calls=%fused_computation.86 | convolution fusion | flops 26550296 | bytes 3047424 | tf_op jit(solution)/shard_map/hst,thd->shd/dot_general | solution.py:16
  123.3 6.2 %collective-permute-done.4 = bf16[128,4096]{0,1:T(8,128)(2,1)} collective-permute-done((bf16[128,4096]{0,1:T(8,128)(2,1)}, bf16[128,4096]{0,1:T(8,128)(2,1)}, u32[]{:S(2)}, u32[]{:S(2)}) %collective-permute-start.4) | collective-permute-done | bytes 1048608 | tf_op jit(solution)/shard_map/ppermute | solution.py:12
  129.6 3.3 %convolution_bitcast_fusion = f32[24,64,64]{2,0,1:T(8,128)} fusion(bf16[128,64,64]{0,2,1:T(8,128)(2,1)} %bitcast.26, f32[64,128]{1,0:T(8,128)S(1)} %copy-done.17, f32[64,24,128]{2,1,0:T(8,128)} %copy-done.14), kind=kOutput, calls=%fused_computation.51 | convolution fusion | flops 25763864 | bytes 2260992 | tf_op jit(solution)/shard_map/hst,thd->shd/dot_general | solution.py:16
  132.9 1.7 convolution_bitcast_fusion.3
  135.9 1.6 fusion.72
  137.6 2.9 %fusion.59 = bf16[24,64,64]{2,0,1:T(8,128)(2,1)S(1)} fusion(f32[24,64,64]{2,0,1:T(8,128)} %convolution_bitcast_fusion, f32[24,64,64]{2,0,1:T(8,128)} %convolution_bitcast_fusion.1, bf16[128,64,64]{0,2,1:T(8,128)(2,1)} %bitcast.19, f32[64,128]{1,0:T(8,128)S(1)} %copy-done.18, f32[64,24,128]{2,1,0:T(8,128)} %copy-done.10), kind=kOutput, calls=%fused_computation.79 | convolution fusion | flops 26058776 | bytes 2850816 | tf_op jit(solution)/shard_map/hst,thd->shd/dot_general | solution.py:16
  140.9 2.8 %copy.61 = bf16[1,1,24,4096]{2,1,0,3:T(2,128)(2,1)S(1)} copy(bf16[1,1,24,4096]{3,2,1,0:T(8,128)(2,1)S(1)} %convert_element_type.128) | data formatting | bytes 393216 | tf_op jit(solution)/shard_map/convert_element_type | solution.py:106
  144.2 23.5 %reduce.6 = bf16[4096,24]{1,0:T(8,128)(2,1)} reduce(bf16[4096,1,1,24]{3,2,1,0:T(2,128)(2,1)S(1)} %bitcast.126, bf16[]{:T(256)} %broadcast.122), dimensions={1,2}, to_apply=%bitcast.103.reduce_sub_computation | reduce | bytes 393218
  167.7 3.4 %reshape.199 = bf16[8,2,6144]{2,1,0:T(2,128)(2,1)} reshape(bf16[4096,24]{1,0:T(8,128)(2,1)} %reduce.6) | data formatting | bytes 393216
  171.0 4.1 %all-to-all-start.3 = ((bf16[8,2,6144]{2,1,0:T(2,128)(2,1)}), bf16[8,2,6144]{2,1,0:T(2,128)(2,1)S(1)}, u32[]{:S(2)}, u32[]{:S(2)}) async-start(bf16[8,2,6144]{2,1,0:T(2,128)(2,1)} %reshape.199), calls=%async_computation.3 | async-start | bytes 393216 | tf_op jit(solution)/shard_map/all_to_all | solution.py:105
  175.1 3.0 %fusion.60 = bf16[24,64,64]{2,0,1:T(8,128)(2,1)S(1)} fusion(f32[64,64,24]{1,2,0:T(8,128)} %fusion.72, f32[64,64,24]{1,2,0:T(8,128)} %fusion.67, bf16[128,64,64]{0,2,1:T(8,128)(2,1)S(1)} %bitcast.131, f32[64,24,128]{2,1,0:T(8,128)} %fusion.86, f32[64,24,128]{2,1,0:T(8,128)} %get-tuple-element.18, f32[64,128]{1,0:T(8,128)S(1)} %copy-done.18), kind=kOutput, calls=%fused_computation.80 | convolution fusion | flops 26845208 | bytes 3637248 | tf_op jit(solution)/shard_map/hst,thd->shd/dot_general | solution.py:16
  178.6 2.8 %copy.58 = bf16[1,1,24,4096]{2,1,0,3:T(2,128)(2,1)S(1)} copy(bf16[1,1,24,4096]{3,2,1,0:T(8,128)(2,1)S(1)} %convert_element_type.125) | data formatting | bytes 393216 | tf_op jit(solution)/shard_map/convert_element_type | solution.py:99
  181.4 22.4 %reduce.5 = bf16[4096,24]{1,0:T(8,128)(2,1)S(1)} reduce(bf16[4096,1,1,24]{3,2,1,0:T(2,128)(2,1)S(1)} %bitcast.127, bf16[]{:T(256)} %broadcast.122), dimensions={1,2}, to_apply=%bitcast.101.reduce_sub_computation | reduce | bytes 393218
  203.8 2.0 reshape.197
  205.8 4.2 %all-to-all-start.2 = ((bf16[8,2,6144]{2,1,0:T(2,128)(2,1)}), bf16[8,2,6144]{2,1,0:T(2,128)(2,1)S(1)}, u32[]{:S(2)}, u32[]{:S(2)}) async-start(bf16[8,2,6144]{2,1,0:T(2,128)(2,1)} %reshape.197), calls=%async_computation.2 | async-start | bytes 393216 | tf_op jit(solution)/shard_map/all_to_all | solution.py:98
  210.0 19.6 %psum.7 = f32[1,4096]{1,0:T(1,128)} all-reduce(f32[1,4096]{1,0:T(1,128)S(1)} %bitcast.149), channel_id=1, replica_groups=mesh['section'=8,'dp'=4] {'dp'}, use_global_device_ids=true, to_apply=%region_17.0 | all-reduce | flops 4096 | bytes 32768 | tf_op jit(solution)/shard_map/psum | solution.py:113
  229.6 3.0 %reshape.200 = bf16[4096,1,1,24]{3,2,1,0:T(2,128)(2,1)S(1)} reshape(bf16[8,2,6144]{2,1,0:T(2,128)(2,1)S(1)} %all-to-all-done.3) | data formatting | bytes 393216
  232.6 2.1 copy.62
  235.5 3.0 %reshape.198 = bf16[4096,1,1,24]{3,2,1,0:T(2,128)(2,1)S(1)} reshape(bf16[8,2,6144]{2,1,0:T(2,128)(2,1)S(1)} %all-to-all-done.2) | data formatting | bytes 393216
  238.5 2.1 copy.59
  (91 shorter events, 13.1 us)
Async XLA Ops:
  0.6 11.4 %all-to-all-start = ((bf16[1,8,24,512]{3,2,0,1:T(8,128)(2,1)}), bf16[1,8,24,512]{3,2,0,1:T(8,128)(2,1)S(1)}, u32[]{:S(2)}, u32[]{:S(2)}) async-start(bf16[1,8,24,512]{3,2,0,1:T(8,128)(2,1)} %bitcast.148), calls=%async_computation | async-start | bytes 393216 | tf_op jit(solution)/shard_map/all_to_all | solution.py:70
  7.8 14.3 %copy-start.19 = (f32[64,64]{1,0:T(8,128)}, f32[64,64]{1,0:T(8,128)S(1)}, u32[]{:S(2)}) copy-start(f32[64,64]{1,0:T(8,128)S(1)} %mul.98) | copy-start | bytes 49156
  12.0 9.5 %all-to-all-start.1 = ((bf16[1,8,24,512]{3,2,0,1:T(8,128)(2,1)}), bf16[1,8,24,512]{3,2,0,1:T(8,128)(2,1)S(1)}, u32[]{:S(2)}, u32[]{:S(2)}) async-start(bf16[1,8,24,512]{3,2,0,1:T(8,128)(2,1)} %bitcast.6), calls=%async_computation.1 | async-start | bytes 393216 | tf_op jit(solution)/shard_map/all_to_all | solution.py:71
  15.5 7.4 %copy-start.25 = (f32[128]{0:T(128)}, f32[128]{0:T(128)S(1)}, u32[]{:S(2)}) copy-start(f32[128]{0:T(128)S(1)} %add_rsqrt_fusion.2) | copy-start | bytes 1540
  21.9 2.7 %copy-start.6 = (bf16[24,64,64]{2,1,0:T(8,128)(2,1)}, bf16[24,64,64]{2,1,0:T(8,128)(2,1)S(1)}, u32[]{:S(2)}) copy-start(bf16[24,64,64]{2,1,0:T(8,128)(2,1)S(1)} %reshape_squeeze.4) | copy-start | bytes 589828
  22.9 1.8 copy-start.14
  27.9 24.9 %copy-start.12 = (f32[1,4096]{1,0:T(1,128)S(1)}, f32[1,4096]{1,0:T(1,128)}, u32[]{:S(2)}) copy-start(f32[1,4096]{1,0:T(1,128)} %param.8) | copy-start | bytes 49156
  27.9 24.3 %collective-permute-start = (bf16[128,4096]{0,1:T(8,128)(2,1)}, bf16[128,4096]{0,1:T(8,128)(2,1)S(1)}, u32[]{:S(2)}, u32[]{:S(2)}) collective-permute-start(bf16[128,4096]{0,1:T(8,128)(2,1)} %fusion.31), channel_id=1, source_target_pairs={{0,4},{4,8},{8,12},{12,16},{16,20},{20,24},{24,28},{28,0},{1,5},{5... | collective-permute-start | bytes 3145736 | tf_op jit(solution)/shard_map/ppermute | solution.py:12
  30.2 23.4 %copy-start.7 = (bf16[24,64,64]{2,1,0:T(8,128)(2,1)S(1)}, bf16[24,64,64]{2,1,0:T(8,128)(2,1)}, u32[]{:S(2)}) copy-start(bf16[24,64,64]{2,1,0:T(8,128)(2,1)} %copy-done.6) | copy-start | bytes 589828
  30.2 31.6 %collective-permute-start.2 = (bf16[128,4096]{0,1:T(8,128)(2,1)}, bf16[128,4096]{0,1:T(8,128)(2,1)}, u32[]{:S(2)}, u32[]{:S(2)}) collective-permute-start(bf16[128,4096]{0,1:T(8,128)(2,1)} %bitcast.18), channel_id=1, source_target_pairs={{0,28},{4,0},{8,4},{12,8},{16,12},{20,16},{24,20},{28,24},{1,29},{... | collective-permute-start | bytes 3145736 | tf_op jit(solution)/shard_map/ppermute | solution.py:12
  52.8 0.7 copy-start.21
  53.5 6.4 %copy-start.4 = (bf16[128,4096]{0,1:T(8,128)(2,1)}, bf16[128,4096]{0,1:T(8,128)(2,1)S(1)}, u32[]{:S(2)}) copy-start(bf16[128,4096]{0,1:T(8,128)(2,1)S(1)} %fusion.22) | copy-start | bytes 3145732
  54.0 0.9 copy-start.11
  61.7 15.2 %collective-permute-start.1 = (bf16[128,4096]{0,1:T(8,128)(2,1)S(1)}, bf16[128,4096]{0,1:T(8,128)(2,1)S(1)}, u32[]{:S(2)}, u32[]{:S(2)}) collective-permute-start(bf16[128,4096]{0,1:T(8,128)(2,1)S(1)} %fusion.30), channel_id=1, source_target_pairs={{0,4},{4,8},{8,12},{12,16},{16,20},{20,24},{24,28},{28,0},{1,5},{5... | collective-permute-start | bytes 3145736 | tf_op jit(solution)/shard_map/ppermute | solution.py:12
  64.4 14.8 %copy-start.8 = (bf16[24,64,64]{2,1,0:T(8,128)(2,1)S(1)}, bf16[24,64,64]{2,1,0:T(8,128)(2,1)}, u32[]{:S(2)}) copy-start(bf16[24,64,64]{2,1,0:T(8,128)(2,1)} %copy-done.6) | copy-start | bytes 589828
  77.4 0.7 copy-start.23
  78.2 1.0 copy-start.2
  79.6 0.9 copy-start.10
  86.2 3.3 %copy-start = (f32[64,128,64]{1,2,0:T(8,128)S(1)}, f32[64,128,64]{1,2,0:T(8,128)}, u32[]{:S(2)}) copy-start(f32[64,128,64]{1,2,0:T(8,128)} %fusion.61) | copy-start | bytes 6291460
  86.2 3.3 %copy-start.24 = (f32[128]{0:T(128)S(1)}, f32[128]{0:T(128)}, u32[]{:S(2)}) copy-start(f32[128]{0:T(128)} %copy-done.23) | copy-start | bytes 1540
  91.4 12.4 %collective-permute-start.3 = (bf16[128,4096]{0,1:T(8,128)(2,1)S(1)}, bf16[128,4096]{0,1:T(8,128)(2,1)S(1)}, u32[]{:S(2)}, u32[]{:S(2)}) collective-permute-start(bf16[128,4096]{0,1:T(8,128)(2,1)S(1)} %fusion.19), channel_id=1, source_target_pairs={{0,28},{4,0},{8,4},{12,8},{16,12},{20,16},{24,20},{28,24},{1,29},{... | collective-permute-start | bytes 3145736 | tf_op jit(solution)/shard_map/ppermute | solution.py:12
  109.1 3.3 %copy-start.1 = (f32[64,128,64]{1,2,0:T(8,128)S(1)}, f32[64,128,64]{1,2,0:T(8,128)}, u32[]{:S(2)}) copy-start(f32[64,128,64]{1,2,0:T(8,128)} %fusion.66) | copy-start | bytes 6291460
  109.1 3.3 %copy-start.22 = (f32[128]{0:T(128)S(1)}, f32[128]{0:T(128)}, u32[]{:S(2)}) copy-start(f32[128]{0:T(128)} %copy-done.21) | copy-start | bytes 1540
  114.2 5.8 %copy-start.5 = (bf16[128,4096]{0,1:T(8,128)(2,1)S(1)}, bf16[128,4096]{0,1:T(8,128)(2,1)}, u32[]{:S(2)}) copy-start(bf16[128,4096]{0,1:T(8,128)(2,1)} %copy-done.4) | copy-start | bytes 3145732
  114.2 15.4 %collective-permute-start.4 = (bf16[128,4096]{0,1:T(8,128)(2,1)}, bf16[128,4096]{0,1:T(8,128)(2,1)}, u32[]{:S(2)}, u32[]{:S(2)}) collective-permute-start(bf16[128,4096]{0,1:T(8,128)(2,1)} %fusion.27), channel_id=1, source_target_pairs={{0,28},{4,0},{8,4},{12,8},{16,12},{20,16},{24,20},{28,24},{1,29},{... | collective-permute-start | bytes 3145736 | tf_op jit(solution)/shard_map/ppermute | solution.py:12
  119.9 9.7 %copy-start.17 = (f32[64,128]{1,0:T(8,128)S(1)}, f32[64,128]{1,0:T(8,128)}, u32[]{:S(2)}) copy-start(f32[64,128]{1,0:T(8,128)} %get-tuple-element.13) | copy-start | bytes 98308
  132.9 1.8 copy-start.9
  132.9 1.8 copy-start.13
  132.9 1.8 copy-start.26
  134.7 1.2 copy-start.20
  135.8 1.7 copy-start.18
  144.2 30.9 %copy-start.3 = (bf16[128,4096]{0,1:T(8,128)(2,1)S(1)}, bf16[128,4096]{0,1:T(8,128)(2,1)}, u32[]{:S(2)}) copy-start(bf16[128,4096]{0,1:T(8,128)(2,1)} %copy-done.2) | copy-start | bytes 3145732
  171.0 34.8 %all-to-all-start.3 = ((bf16[8,2,6144]{2,1,0:T(2,128)(2,1)}), bf16[8,2,6144]{2,1,0:T(2,128)(2,1)S(1)}, u32[]{:S(2)}, u32[]{:S(2)}) async-start(bf16[8,2,6144]{2,1,0:T(2,128)(2,1)} %reshape.199), calls=%async_computation.3 | async-start | bytes 393216 | tf_op jit(solution)/shard_map/all_to_all | solution.py:105
  181.3 28.7 %copy-start.15 = (f32[4096]{0:T(1024)S(1)}, f32[4096]{0:T(1024)}, u32[]{:S(2)}) copy-start(f32[4096]{0:T(1024)} %get-tuple-element.11) | copy-start | bytes 49156
  181.4 28.6 %copy-start.16 = (f32[4096]{0:T(1024)S(1)}, f32[4096]{0:T(1024)}, u32[]{:S(2)}) copy-start(f32[4096]{0:T(1024)} %get-tuple-element.9) | copy-start | bytes 49156
  205.8 29.7 %all-to-all-start.2 = ((bf16[8,2,6144]{2,1,0:T(2,128)(2,1)}), bf16[8,2,6144]{2,1,0:T(2,128)(2,1)S(1)}, u32[]{:S(2)}, u32[]{:S(2)}) async-start(bf16[8,2,6144]{2,1,0:T(2,128)(2,1)} %reshape.197), calls=%async_computation.2 | async-start | bytes 393216 | tf_op jit(solution)/shard_map/all_to_all | solution.py:98
where the time goes:
time: 242 us; the launch traced here: 241 us
  other arithmetic  68.8 us (28%)
  waiting for transfers between devices  58.5 us (24%)
  matrix products  39 us (16%)
  local copies, waits for them, and re-layouts  32 us (13%)
  starting transfers between devices  22.4 us (9%)
  blocking collectives  19.6 us (8%)
    ppermute x5, waiting for transfers between devices, from_behind(): lax.ppermute(x, axis, [(i, (i + by) % length) for i in range(length)])  50.5 us
    unnamed x3, other arithmetic  47.3 us
    dot_general x17, matrix products, product(): return jnp.einsum(form, left, right, preferred_element_type=jnp.float32)  39 us
    unnamed x66, local copies, waits for them, and re-layouts  20.7 us
    psum x1, blocking collectives, on_device(): gain_summed = lax.psum(gain_total, 'dp')  19.6 us
    reduce_sum x2, other arithmetic, attend_backward(): gain_step = jnp.sum(dquery * unit, axis=0)  6.51 us
    all_to_all x1, waiting for transfers between devices, on_device(): lax.all_to_all(value_rows, 'section', split_axis=1, concat_axis=3, tiled=...  6.05 us
    ppermute x5, starting transfers between devices, from_behind(): lax.ppermute(x, axis, [(i, (i + by) % length) for i in range(length)])  5.55 us
  transfers between devices with their start and end apart: 9, of which 6 were waited for; matrix products, arithmetic and copies ran while one was open for 25% of the time, Pallas kernels for 0%

commit v1 on v0

v1 whole, which is shorter than its diff:
```python
import functools

import jax
import jax.numpy as jnp
from jax import lax
from jax.experimental import pallas as pl
from jax.experimental.pallas import tpu as pltpu
from jax.sharding import PartitionSpec as P

HEAD = 64
TICKS = 3
LANES = 128
MESH = pl.DeviceIdType.MESH
F32 = jnp.float32
BF16 = jnp.bfloat16


def nn(a, b):
    return lax.dot_general(a, b, (((1,), (0,)), ((), ())), preferred_element_type=F32)


def nt(a, b):
    return lax.dot_general(a, b, (((1,), (1,)), ((), ())), preferred_element_type=F32)


def kernel(
    n, ndp, unroll,
    x_ref, ct_ref, k_ref, v_ref, g_ref,
    kout_ref, vout_ref, gout_ref,
    xin, cin, gin, stat, kd, vd, kdt, vdt, gt, xs, qs, probs, plow, raws, ds, grads,
    red, inv, ar, ktot, vtot, gsend, gmid, gdp,
    x_send, x_recv, c_send, c_recv, g_send, g_recv, st_send, st_recv,
    ar_send, ar_recv, gm_send, gm_recv, dp_send, dp_recv, loc,
):
    me = lax.axis_index("section")
    doc = lax.axis_index("dp")
    tok, width = x_ref.shape
    src, cols = k_ref.shape[1], k_ref.shape[2]
    blocks = cols // LANES
    per = LANES // HEAD
    brow = per * src
    scale = HEAD ** (-0.5)

    def peers(body):
        def step(j, c):
            body(lax.rem(me + j, n))
            return c
        lax.fori_loop(1, n, step, 0)

    def docs(body):
        def step(j, c):
            body(lax.rem(doc + j, ndp))
            return c
        lax.fori_loop(1, ndp, step, 0)

    def each(body, u=None):
        def step(m, c):
            body(m)
            return c
        lax.fori_loop(0, n, step, 0, unroll=u or unroll)

    def to(p, source, target, send, recv):
        return pltpu.make_async_remote_copy(
            src_ref=source, dst_ref=target, send_sem=send, recv_sem=recv,
            device_id={"section": p}, device_id_type=MESH)

    def to_doc(p, source, target, send, recv):
        return pltpu.make_async_remote_copy(
            src_ref=source, dst_ref=target, send_sem=send, recv_sem=recv,
            device_id={"dp": p}, device_id_type=MESH)

    def cut(ref, p):
        return ref.at[:, pl.ds(pl.multiple_of(p * cols, LANES), cols)]

    def x_copy(p, slot):
        return to(p, cut(x_ref, p), xin.at[slot], x_send.at[p], x_recv.at[slot])

    def c_copy(p, slot):
        return to(p, cut(ct_ref, p), cin.at[slot], c_send.at[p], c_recv.at[slot])

    def g_copy(p, slot):
        return to(p, cut(g_ref, p), gin.at[slot], g_send.at[p], g_recv.at[slot])

    def st_copy(p, slot):
        return to(p, stat.at[me], stat.at[slot], st_send.at[p], st_recv.at[slot])

    def ar_copy(a, p, slot):
        return to(p, ar.at[a, me], ar.at[a, slot], ar_send.at[a, p], ar_recv.at[a, slot])

    def gm_copy(p, slot):
        return to(p, gsend.at[p], gmid.at[slot], gm_send.at[p], gm_recv.at[slot])

    def dp_copy(p, slot):
        return to_doc(p, gmid, gdp.at[slot], dp_send.at[p], dp_recv.at[slot])

    barrier = pltpu.get_barrier_semaphore()
    peers(lambda p: pl.semaphore_signal(barrier, inc=1, device_id={"section": p}, device_id_type=MESH))
    docs(lambda p: pl.semaphore_signal(barrier, inc=1, device_id={"dp": p}, device_id_type=MESH))
    pl.semaphore_wait(barrier, n + ndp - 2)

    peers(lambda p: g_copy(p, me).start())
    peers(lambda p: x_copy(p, me).start())
    own = [
        pltpu.make_async_copy(cut(g_ref, me), gin.at[me], loc.at[0]),
        pltpu.make_async_copy(cut(x_ref, me), xin.at[me], loc.at[1]),
        pltpu.make_async_copy(cut(ct_ref, me), cin.at[me], loc.at[2]),
    ]
    for copy in own:
        copy.start()

    total = jnp.zeros((tok, LANES), F32)
    for b in range(width // LANES):
        part = x_ref[:, b * LANES:(b + 1) * LANES].astype(F32)
        total = total + part * part
    stat[me] = jnp.sum(total.T, axis=0, keepdims=True)
    peers(lambda p: st_copy(p, me).start())
    peers(lambda p: c_copy(p, me).start())

    lane = lax.broadcasted_iota(jnp.int32, (src, LANES), 1)
    sides = [jnp.logical_and(lane >= i * HEAD, lane < (i + 1) * HEAD) for i in range(per)]

    def spread(l):
        for source, plain, turned in ((k_ref, kd, kdt), (v_ref, vd, vdt)):
            rows = source[l].astype(F32)
            for b in range(blocks):
                piece = rows[:, b * LANES:(b + 1) * LANES]
                both = jnp.concatenate([jnp.where(s, piece, 0.0) for s in sides], axis=0)
                plain[l, b] = both.astype(BF16)
                turned[l, b] = both.T.astype(BF16)
        ktot[l] = jnp.zeros((src, cols), F32)
        vtot[l] = jnp.zeros((src, cols), F32)

    each(spread, 1)

    own[0].wait()
    peers(lambda p: g_copy(p, p).wait_recv())

    def turn_gain(l):
        for b in range(blocks):
            row = gin[l, :, b * LANES:(b + 1) * LANES]
            gt[l, b * LANES:(b + 1) * LANES, :] = jnp.broadcast_to(row, (LANES, LANES)).T

    each(turn_gain, 1)
    stats_done = peers(lambda p: st_copy(p, p).wait_recv())

    def fwd(k, m, more):
        l = lax.rem(m + k, n)
        factor = inv[k, m]
        pieces = []
        sums = jnp.zeros((1, tok), F32)
        for b in range(blocks):
            at = slice(b * LANES, (b + 1) * LANES)
            rows = slice(b * brow, (b + 1) * brow)
            xf = xs[k, m, at, :].astype(F32)
            q = (xf * factor * gt[l, at, :]).astype(BF16)
            qs[k, m, at, :] = q
            raw = nn(kd[l, b], q)
            raws[k, m, rows, :] = raw
            s3 = raw.reshape(per, src, tok) * scale
            w = jnp.exp(s3 - jnp.max(s3, axis=1, keepdims=True))
            p = w * (1.0 / jnp.sum(w, axis=1, keepdims=True))
            p = p.reshape(brow, tok)
            probs[k, m, rows, :] = p
            low = p.astype(BF16)
            plow[k, m, rows, :] = low
            if more:
                y = (xf + nn(vdt[l, b], low)).astype(BF16)
                xs[k + 1, m, at, :] = y
                yf = y.astype(F32)
                sums = sums + jnp.sum(yf * yf, axis=0, keepdims=True)
        if more:
            ar[k, me, m] = sums

    def reduced(a):
        peers(lambda p: ar_copy(a, p, p).wait_recv())
        total = ar[a, 0]
        for s in range(1, n):
            total = total + ar[a, s]
        return total * (1.0 / width)

    def arrive(j, c):
        m = lax.rem(me + j, n)

        @pl.when(j == 0)
        def _():
            own[1].wait()

        @pl.when(j > 0)
        def _():
            x_copy(m, m).wait_recv()

        inv[0, m] = lax.rsqrt(stat[m] * (1.0 / width) + 1e-6)
        for b in range(blocks):
            at = slice(b * LANES, (b + 1) * LANES)
            xs[0, m, at, :] = xin[m, :, at].T
        fwd(0, m, True)
        return c

    lax.fori_loop(0, n, arrive, 0)
    for k in range(1, TICKS):
        peers(lambda p: ar_copy(k - 1, p, me).start())
        inv[k] = lax.rsqrt(reduced(k - 1) + 1e-6)
        each(lambda m: fwd(k, m, k + 1 < TICKS))

    def arrive_c(j, c):
        s = lax.rem(me + j, n)

        @pl.when(j == 0)
        def _():
            own[2].wait()

        @pl.when(j > 0)
        def _():
            c_copy(s, s).wait_recv()

        m = lax.rem(s + TICKS * n - TICKS, n)
        for b in range(blocks):
            at = slice(b * LANES, (b + 1) * LANES)
            grads[m, at, :] = cin[s, :, at].T
        return c

    lax.fori_loop(0, n, arrive_c, 0)

    def scores_back(k, a, m):
        l = lax.rem(m + k, n)
        sums = jnp.zeros((1, tok), F32)
        for b in range(blocks):
            at = slice(b * LANES, (b + 1) * LANES)
            rows = slice(b * brow, (b + 1) * brow)
            dprob = nn(vd[l, b], grads[m, at, :]).reshape(per, src, tok)
            p = probs[k, m, rows, :].reshape(per, src, tok)
            mean = jnp.sum(p * dprob, axis=1, keepdims=True)
            d = (p * (dprob - mean) * scale).reshape(brow, tok).astype(BF16)
            ds[m, rows, :] = d
            if a is not None:
                sums = sums + jnp.sum(d.astype(F32) * raws[k, m, rows, :], axis=0, keepdims=True)
        if a is not None:
            ar[a, me, m] = sums

    def picked(r):
        out = r[:src]
        for i in range(1, per):
            out = jnp.where(sides[i], r[i * src:(i + 1) * src], out)
        return out

    def key_step(k, m):
        l = lax.rem(m + k, n)
        for b in range(blocks):
            at = slice(b * LANES, (b + 1) * LANES)
            rows = slice(b * brow, (b + 1) * brow)
            ktot[l, :, at] += picked(nt(ds[m, rows, :], qs[k, m, at, :]))

    def value_step(k, m):
        l = lax.rem(m + k, n)
        for b in range(blocks):
            at = slice(b * LANES, (b + 1) * LANES)
            rows = slice(b * brow, (b + 1) * brow)
            vtot[l, :, at] += picked(nt(plow[k, m, rows, :], grads[m, at, :]))

    def input_back(k, m):
        l = lax.rem(m + k, n)
        factor = inv[k, m]
        mean = red[m]
        for b in range(blocks):
            at = slice(b * LANES, (b + 1) * LANES)
            rows = slice(b * brow, (b + 1) * brow)
            dq = nn(kdt[l, b], ds[m, rows, :])
            u = xs[k, m, at, :].astype(F32) * factor
            back = grads[m, at, :].astype(F32) + factor * (gt[l, at, :] * dq - u * mean)
            grads[m, at, :] = back.astype(BF16)

    for k in range(TICKS - 1, 0, -1):
        a = TICKS - 1 + k - 1
        each(lambda m: scores_back(k, a, m))
        peers(lambda p: ar_copy(a, p, me).start())

        def filler(m):
            key_step(k, m)
            value_step(k, m)

        each(filler)
        red[...] = reduced(a)
        each(lambda m: input_back(k, m))

    def last(m):
        scores_back(0, None, m)
        key_step(0, m)
        steps = ktot[m]
        kout_ref[m] = steps.astype(BF16)
        gsend[m] = jnp.sum(steps * k_ref[m].astype(F32), axis=0, keepdims=True) / gin[m]

    each(last)
    peers(lambda p: gm_copy(p, me).start())
    gmid[me] = gsend[me]

    def finish(m):
        value_step(0, m)
        vout_ref[m] = vtot[m].astype(BF16)

    each(finish)
    peers(lambda p: gm_copy(p, p).wait_recv())
    docs(lambda p: dp_copy(p, doc).start())

    def drain(p):
        x_copy(p, me).wait_send()
        c_copy(p, me).wait_send()
        g_copy(p, me).wait_send()
        st_copy(p, me).wait_send()
        for a in range(2 * (TICKS - 1)):
            ar_copy(a, p, me).wait_send()
        gm_copy(p, me).wait_send()

    peers(drain)
    gdp[doc] = gmid[...]
    docs(lambda p: dp_copy(p, p).wait_recv())
    docs(lambda p: dp_copy(p, doc).wait_send())
    for s in range(n):
        out = gdp[0, s]
        for d in range(1, ndp):
            out = out + gdp[d, s]
        gout_ref[:, s * cols:(s + 1) * cols] = out


def on_device(inputs, key_rows, value_rows, query_gain, cotangent):
    n = lax.axis_size("section")
    ndp = lax.axis_size("dp")
    tok, width = inputs.shape[2:]
    src, cols = key_rows.shape[2:]
    blocks = cols // LANES
    brow = LANES // HEAD * src
    rows = blocks * brow
    rounds = 2 * (TICKS - 1)
    vmem = pltpu.VMEM
    sem = pltpu.SemaphoreType.DMA
    scratch = [
        vmem((n, tok, cols), BF16), vmem((n, tok, cols), BF16),
        vmem((n, 1, cols), F32), vmem((n, 1, tok), F32),
        vmem((n, blocks, brow, LANES), BF16), vmem((n, blocks, brow, LANES), BF16),
        vmem((n, blocks, LANES, brow), BF16), vmem((n, blocks, LANES, brow), BF16),
        vmem((n, cols, LANES), F32),
        vmem((TICKS, n, cols, tok), BF16), vmem((TICKS, n, cols, tok), BF16),
        vmem((TICKS, n, rows, tok), F32), vmem((TICKS, n, rows, tok), BF16),
        vmem((TICKS, n, rows, tok), F32),
        vmem((n, rows, tok), BF16), vmem((n, cols, tok), BF16),
        vmem((n, 1, tok), F32), vmem((TICKS, n, 1, tok), F32),
        vmem((rounds, n, n, 1, tok), F32),
        vmem((n, src, cols), F32), vmem((n, src, cols), F32),
        vmem((n, 1, cols), F32), vmem((n, 1, cols), F32), vmem((ndp, n, 1, cols), F32),
        sem((n,)), sem((n,)), sem((n,)), sem((n,)), sem((n,)), sem((n,)), sem((n,)), sem((n,)),
        sem((rounds, n)), sem((rounds, n)), sem((n,)), sem((n,)), sem((ndp,)), sem((ndp,)), sem((3,)),
    ]
    in_vmem = pl.BlockSpec(memory_space=pltpu.VMEM)
    in_place = pl.BlockSpec(memory_space=pl.ANY)
    unroll = 2
    keys, values, gains = pl.pallas_call(
        functools.partial(kernel, n, ndp, unroll),
        out_shape=(
            jax.ShapeDtypeStruct((n, src, cols), BF16),
            jax.ShapeDtypeStruct((n, src, cols), BF16),
            jax.ShapeDtypeStruct((1, width), F32),
        ),
        in_specs=[in_vmem, in_place, in_vmem, in_vmem, in_vmem],
        out_specs=(in_vmem, in_vmem, in_vmem),
        scratch_shapes=scratch,
        compiler_params=pltpu.CompilerParams(
            collective_id=0, has_side_effects=True, vmem_limit_bytes=60 * 1024 * 1024),
    )(inputs[0, 0], cotangent[0, 0], key_rows[0], value_rows[0], query_gain)
    return keys[None], values[None], gains


def solution(mesh):
    return jax.shard_map(
        on_device,
        mesh=mesh,
        in_specs=(
            P("dp", "section", None, None),
            P("dp", None, None, "section"),
            P("dp", None, None, "section"),
            P("section", None),
            P("dp", "section", None, None),
        ),
        out_specs=(
            P("dp", None, None, "section"),
            P("dp", None, None, "section"),
            P("section", None),
        ),
        check_vma=False,
    )
```

time: 242 us -> 64.4 us (0.27)
  other arithmetic: 68.8 us -> 0 us
  Pallas kernels: 0 us -> 60.5 us
  waiting for transfers between devices: 58.5 us -> 0 us
  matrix products: 39 us -> 0 us
  local copies, waits for them, and re-layouts: 32 us -> 2.98 us
  starting transfers between devices: 22.4 us -> 0 us
  blocking collectives: 19.6 us -> 0 us
    pallas_call x0 -> x1, Pallas kernels: none -> 60.5 us  [on_device(): pl.pallas_call(functools.partial(kernel, n, ndp, unroll), out_shape=(jax....]
    ppermute x5 -> x0, waiting for transfers between devices: 50.5 us -> none  [from_behind(): lax.ppermute(x, axis, [(i, (i + by) % length) for i in range(length)])]
    unnamed x3 -> x0, other arithmetic: 47.3 us -> none
    dot_general x17 -> x0, matrix products: 39 us -> none  [product(): return jnp.einsum(form, left, right, preferred_element_type=jnp.float32)]
    psum x1 -> x0, blocking collectives: 19.6 us -> none  [on_device(): gain_summed = lax.psum(gain_total, 'dp')]
    unnamed x66 -> x7, local copies, waits for them, and re-layouts: 20.7 us -> 2.98 us
    all_to_all x4 -> x0, starting transfers between devices: 16.9 us -> none  [the longest x1 5.21 us: on_device(): lax.all_to_all(key_rows, 'section', split_axis=1, concat_axis=3, tiled=True)]
    reduce_sum x5 -> x0, other arithmetic: 8.18 us -> none  [the longest x2 6.51 us: attend_backward(): gain_step = jnp.sum(dquery * unit, axis=0)]
  transfers between devices with their start and end apart: 9 -> 0, of which waited for: 6 -> 0; matrix products, arithmetic and copies ran while one was open for 25% -> 0% of each run, Pallas kernels for 0% -> 0%
where the time goes in v1:
time: 64.4 us; the launch traced here: 64.1 us
  Pallas kernels  60.5 us (94%)
  local copies, waits for them, and re-layouts  2.98 us (5%)
  between operations  0.65 us (1%)
    pallas_call x1, Pallas kernels, on_device(): pl.pallas_call(functools.partial(kernel, n, ndp, unroll), out_shape=(jax....  60.5 us
    unnamed x7, local copies, waits for them, and re-layouts  2.98 us

profile of v1, /device:TPU:0, one launch (start us, length us, event | category | flops | bytes accessed | tf_op | source)
XLA Modules:
  0.0 64.1 jit_solution(13831321761230431293)
XLA Ops:
  0.6 60.5 %shard_map.76 = (bf16[8,24,512]{2,1,0:T(8,128)(2,1)}, bf16[8,24,512]{2,1,0:T(8,128)(2,1)}, f32[1,4096]{1,0:T(1,128)}) custom-call(bf16[128,4096]{1,0:T(8,128)(2,1)} %bitcast.6, bf16[128,4096]{1,0:T(8,128)(2,1)} %bitcast.7, bf16[8,24,512]{2,1,0:T(8,128)(2,1)} %bitcast.8, bf16[8,24,512]{2,1,0:T(8,128)(2,1)} %bitcast.9, f32[1,4096]{1,0:T(1,128)} %g_ref.1), custom_call_target="tpu_custom_call" | custom-call | tf_op jit(solution)/shard_map/pallas_call | solution.py:355
  61.1 0.0 copy-start
  61.2 1.7 %copy.11 = bf16[1,8,24,512]{3,2,1,0:T(8,128)(2,1)} copy(bf16[1,8,24,512]{3,2,1,0:T(8,128)(2,1)} %bitcast.11) | data formatting | bytes 393216
  62.8 0.0 copy-done
  62.8 0.0 copy-start.1
  62.8 0.7 %copy.12 = bf16[1,8,24,512]{3,2,1,0:T(8,128)(2,1)} copy(bf16[1,8,24,512]{3,2,1,0:T(8,128)(2,1)S(1)} %bitcast.10) | data formatting | bytes 393216
  63.5 0.0 copy-done.1
  63.5 0.6 copy.13
Async XLA Ops:
  61.1 1.7 %copy-start = (bf16[8,24,512]{2,1,0:T(8,128)(2,1)S(1)}, bf16[8,24,512]{2,1,0:T(8,128)(2,1)}, u32[]{:S(2)}) copy-start(bf16[8,24,512]{2,1,0:T(8,128)(2,1)} %get-tuple-element.7) | copy-start | bytes 589828
  62.8 0.7 %copy-start.1 = (f32[1,4096]{1,0:T(1,128)S(1)}, f32[1,4096]{1,0:T(1,128)}, u32[]{:S(2)}) copy-start(f32[1,4096]{1,0:T(1,128)} %get-tuple-element.14) | copy-start | bytes 49156

commit v2 on v1

--- a/solution.py
+++ b/solution.py
@@ -41,11 +41,11 @@
     brow = per * src
     scale = HEAD ** (-0.5)
 
-    def peers(body):
+    def peers(body, first=1, last=n):
         def step(j, c):
             body(lax.rem(me + j, n))
             return c
-        lax.fori_loop(1, n, step, 0)
+        lax.fori_loop(first, last, step, 0)
 
     def docs(body):
         def step(j, c):
@@ -53,11 +53,14 @@
             return c
         lax.fori_loop(1, ndp, step, 0)
 
-    def each(body, u=None):
+    def each(body, first=0, last=n, u=None):
         def step(m, c):
             body(m)
             return c
-        lax.fori_loop(0, n, step, 0, unroll=u or unroll)
+        lax.fori_loop(first, last, step, 0, unroll=u or min(unroll, last - first))
+
+    half = n // 2
+    halves = ((0, half), (half, n))
 
     def to(p, source, target, send, recv):
         return pltpu.make_async_remote_copy(
@@ -84,8 +87,12 @@
     def st_copy(p, slot):
         return to(p, stat.at[me], stat.at[slot], st_send.at[p], st_recv.at[slot])
 
-    def ar_copy(a, p, slot):
-        return to(p, ar.at[a, me], ar.at[a, slot], ar_send.at[a, p], ar_recv.at[a, slot])
+    def ar_copy(a, h, p, slot):
+        lo, hi = halves[h]
+        return to(p, ar.at[a, me, lo:hi], ar.at[a, slot, lo:hi], ar_send.at[a, h, p], ar_recv.at[a, h, slot])
+
+    def share(a, h):
+        peers(lambda p: ar_copy(a, h, p, me).start())
 
     def gm_copy(p, slot):
         return to(p, gsend.at[p], gmid.at[slot], gm_send.at[p], gm_recv.at[slot])
@@ -96,10 +103,20 @@
     barrier = pltpu.get_barrier_semaphore()
     peers(lambda p: pl.semaphore_signal(barrier, inc=1, device_id={"section": p}, device_id_type=MESH))
     docs(lambda p: pl.semaphore_signal(barrier, inc=1, device_id={"dp": p}, device_id_type=MESH))
+
+    total = jnp.zeros((tok, LANES), F32)
+    for b in range(width // LANES):
+        part = x_ref[:, b * LANES:(b + 1) * LANES].astype(F32)
+        total = total + part * part
+    stat[me] = jnp.sum(total.T, axis=0, keepdims=True)
+
     pl.semaphore_wait(barrier, n + ndp - 2)
 
     peers(lambda p: g_copy(p, me).start())
+    peers(lambda p: st_copy(p, me).start())
     peers(lambda p: x_copy(p, me).start())
+    first_cut, second_cut = (1 + n) // 4, 1 + (5 * n) // 8
+    peers(lambda p: c_copy(p, me).start(), 1, first_cut)
     own = [
         pltpu.make_async_copy(cut(g_ref, me), gin.at[me], loc.at[0]),
         pltpu.make_async_copy(cut(x_ref, me), xin.at[me], loc.at[1]),
@@ -107,14 +124,6 @@
     ]
     for copy in own:
         copy.start()
-
-    total = jnp.zeros((tok, LANES), F32)
-    for b in range(width // LANES):
-        part = x_ref[:, b * LANES:(b + 1) * LANES].astype(F32)
-        total = total + part * part
-    stat[me] = jnp.sum(total.T, axis=0, keepdims=True)
-    peers(lambda p: st_copy(p, me).start())
-    peers(lambda p: c_copy(p, me).start())
 
     lane = lax.broadcasted_iota(jnp.int32, (src, LANES), 1)
     sides = [jnp.logical_and(lane >= i * HEAD, lane < (i + 1) * HEAD) for i in range(per)]
@@ -130,7 +139,7 @@
         ktot[l] = jnp.zeros((src, cols), F32)
         vtot[l] = jnp.zeros((src, cols), F32)
 
-    each(spread, 1)
+    each(spread, u=2)
 
     own[0].wait()
     peers(lambda p: g_copy(p, p).wait_recv())
@@ -140,8 +149,8 @@
             row = gin[l, :, b * LANES:(b + 1) * LANES]
             gt[l, b * LANES:(b + 1) * LANES, :] = jnp.broadcast_to(row, (LANES, LANES)).T
 
-    each(turn_gain, 1)
-    stats_done = peers(lambda p: st_copy(p, p).wait_recv())
+    each(turn_gain, u=2)
+    peers(lambda p: st_copy(p, p).wait_recv())
 
     def fwd(k, m, more):
         l = lax.rem(m + k, n)
@@ -171,11 +180,12 @@
         if more:
             ar[k, me, m] = sums
 
-    def reduced(a):
-        peers(lambda p: ar_copy(a, p, p).wait_recv())
-        total = ar[a, 0]
+    def reduced(a, h):
+        lo, hi = halves[h]
+        peers(lambda p: ar_copy(a, h, p, p).wait_recv())
+        total = ar[a, 0, lo:hi]
         for s in range(1, n):
-            total = total + ar[a, s]
+            total = total + ar[a, s, lo:hi]
         return total * (1.0 / width)
 
     def arrive(j, c):
@@ -197,29 +207,30 @@
         return c
 
     lax.fori_loop(0, n, arrive, 0)
+    share(0, 0)
+    share(0, 1)
+    peers(lambda p: c_copy(p, me).start(), first_cut, second_cut)
     for k in range(1, TICKS):
-        peers(lambda p: ar_copy(k - 1, p, me).start())
-        inv[k] = lax.rsqrt(reduced(k - 1) + 1e-6)
-        each(lambda m: fwd(k, m, k + 1 < TICKS))
-
-    def arrive_c(j, c):
-        s = lax.rem(me + j, n)
-
-        @pl.when(j == 0)
-        def _():
-            own[2].wait()
-
-        @pl.when(j > 0)
-        def _():
-            c_copy(s, s).wait_recv()
-
-        m = lax.rem(s + TICKS * n - TICKS, n)
-        for b in range(blocks):
-            at = slice(b * LANES, (b + 1) * LANES)
-            grads[m, at, :] = cin[s, :, at].T
-        return c
-
-    lax.fori_loop(0, n, arrive_c, 0)
+        for h, (lo, hi) in enumerate(halves):
+            inv[k, lo:hi] = lax.rsqrt(reduced(k - 1, h) + 1e-6)
+            each(lambda m: fwd(k, m, k + 1 < TICKS), lo, hi)
+            if k + 1 < TICKS:
+                share(k, h)
+        if k == 1:
+            peers(lambda p: c_copy(p, me).start(), second_cut, n)
+
+    own[2].wait()
+
+    def arrive_c(p):
+        c_copy(p, p).wait_recv()
+
+    def turn_c(m):
+        s = lax.rem(m + TICKS, n)
+        for b in range(blocks):
+            at = slice(b * LANES, (b + 1) * LANES)
+            grads[TICKS - 1, m, at, :] = cin[s, :, at].T
+
+    peers(arrive_c)
 
     def scores_back(k, a, m):
         l = lax.rem(m + k, n)
@@ -227,11 +238,11 @@
         for b in range(blocks):
             at = slice(b * LANES, (b + 1) * LANES)
             rows = slice(b * brow, (b + 1) * brow)
-            dprob = nn(vd[l, b], grads[m, at, :]).reshape(per, src, tok)
+            dprob = nn(vd[l, b], grads[k, m, at, :]).reshape(per, src, tok)
             p = probs[k, m, rows, :].reshape(per, src, tok)
             mean = jnp.sum(p * dprob, axis=1, keepdims=True)
             d = (p * (dprob - mean) * scale).reshape(brow, tok).astype(BF16)
-            ds[m, rows, :] = d
+            ds[k, m, rows, :] = d
             if a is not None:
                 sums = sums + jnp.sum(d.astype(F32) * raws[k, m, rows, :], axis=0, keepdims=True)
         if a is not None:
@@ -248,14 +259,14 @@
         for b in range(blocks):
             at = slice(b * LANES, (b + 1) * LANES)
             rows = slice(b * brow, (b + 1) * brow)
-            ktot[l, :, at] += picked(nt(ds[m, rows, :], qs[k, m, at, :]))
+            ktot[l, :, at] += picked(nt(ds[k, m, rows, :], qs[k, m, at, :]))
 
     def value_step(k, m):
         l = lax.rem(m + k, n)
         for b in range(blocks):
             at = slice(b * LANES, (b + 1) * LANES)
             rows = slice(b * brow, (b + 1) * brow)
-            vtot[l, :, at] += picked(nt(plow[k, m, rows, :], grads[m, at, :]))
+            vtot[l, :, at] += picked(nt(plow[k, m, rows, :], grads[k, m, at, :]))
 
     def input_back(k, m):
         l = lax.rem(m + k, n)
@@ -264,26 +275,33 @@
         for b in range(blocks):
             at = slice(b * LANES, (b + 1) * LANES)
             rows = slice(b * brow, (b + 1) * brow)
-            dq = nn(kdt[l, b], ds[m, rows, :])
+            dq = nn(kdt[l, b], ds[k, m, rows, :])
             u = xs[k, m, at, :].astype(F32) * factor
-            back = grads[m, at, :].astype(F32) + factor * (gt[l, at, :] * dq - u * mean)
-            grads[m, at, :] = back.astype(BF16)
-
+            back = grads[k, m, at, :].astype(F32) + factor * (gt[l, at, :] * dq - u * mean)
+            grads[k - 1, m, at, :] = back.astype(BF16)
+
+    def start_back(m):
+        turn_c(m)
+        scores_back(TICKS - 1, 2 * TICKS - 3, m)
+
+    for h, (lo, hi) in enumerate(halves):
+        each(start_back, lo, hi)
+        share(2 * TICKS - 3, h)
     for k in range(TICKS - 1, 0, -1):
         a = TICKS - 1 + k - 1
-        each(lambda m: scores_back(k, a, m))
-        peers(lambda p: ar_copy(a, p, me).start())
-
-        def filler(m):
-            key_step(k, m)
-            value_step(k, m)
-
-        each(filler)
-        red[...] = reduced(a)
-        each(lambda m: input_back(k, m))
+
+        def next_back(m):
+            input_back(k, m)
+            scores_back(k - 1, a - 1 if k > 1 else None, m)
+
+        each(lambda m: key_step(k, m))
+        for h, (lo, hi) in enumerate(halves):
+            red[lo:hi] = reduced(a, h)
+            each(next_back, lo, hi)
+            if k > 1:
+                share(a - 1, h)
 
     def last(m):
-        scores_back(0, None, m)
         key_step(0, m)
         steps = ktot[m]
         kout_ref[m] = steps.astype(BF16)
@@ -293,13 +311,17 @@
     peers(lambda p: gm_copy(p, me).start())
     gmid[me] = gsend[me]
 
+    each(lambda m: value_step(TICKS - 1, m))
+    for k in range(1, TICKS - 1):
+        each(lambda m: value_step(k, m))
+    peers(lambda p: gm_copy(p, p).wait_recv())
+    docs(lambda p: dp_copy(p, doc).start())
+
     def finish(m):
         value_step(0, m)
         vout_ref[m] = vtot[m].astype(BF16)
 
     each(finish)
-    peers(lambda p: gm_copy(p, p).wait_recv())
-    docs(lambda p: dp_copy(p, doc).start())
 
     def drain(p):
         x_copy(p, me).wait_send()
@@ -307,7 +329,8 @@
         g_copy(p, me).wait_send()
         st_copy(p, me).wait_send()
         for a in range(2 * (TICKS - 1)):
-            ar_copy(a, p, me).wait_send()
+            for h in range(2):
+                ar_copy(a, h, p, me).wait_send()
         gm_copy(p, me).wait_send()
 
     peers(drain)
@@ -341,17 +364,17 @@
         vmem((TICKS, n, cols, tok), BF16), vmem((TICKS, n, cols, tok), BF16),
         vmem((TICKS, n, rows, tok), F32), vmem((TICKS, n, rows, tok), BF16),
         vmem((TICKS, n, rows, tok), F32),
-        vmem((n, rows, tok), BF16), vmem((n, cols, tok), BF16),
+        vmem((TICKS, n, rows, tok), BF16), vmem((TICKS, n, cols, tok), BF16),
         vmem((n, 1, tok), F32), vmem((TICKS, n, 1, tok), F32),
         vmem((rounds, n, n, 1, tok), F32),
         vmem((n, src, cols), F32), vmem((n, src, cols), F32),
         vmem((n, 1, cols), F32), vmem((n, 1, cols), F32), vmem((ndp, n, 1, cols), F32),
         sem((n,)), sem((n,)), sem((n,)), sem((n,)), sem((n,)), sem((n,)), sem((n,)), sem((n,)),
-        sem((rounds, n)), sem((rounds, n)), sem((n,)), sem((n,)), sem((ndp,)), sem((ndp,)), sem((3,)),
+        sem((rounds, 2, n)), sem((rounds, 2, n)), sem((n,)), sem((n,)), sem((ndp,)), sem((ndp,)), sem((3,)),
     ]
     in_vmem = pl.BlockSpec(memory_space=pltpu.VMEM)
     in_place = pl.BlockSpec(memory_space=pl.ANY)
-    unroll = 2
+    unroll = 8
     keys, values, gains = pl.pallas_call(
         functools.partial(kernel, n, ndp, unroll),
         out_shape=(

time: 64.4 us -> 60.9 us (0.946)
  Pallas kernels: 60.5 us -> 57 us
    pallas_call x1, Pallas kernels: 60.5 us -> 57 us  [on_device(): pl.pallas_call(functools.partial(kernel, n, ndp, unroll), out_shape=(jax....]
where the time goes in v2:
time: 60.9 us; the launch traced here: 60.6 us
  Pallas kernels  57 us (94%)
  local copies, waits for them, and re-layouts  2.98 us (5%)
  between operations  0.65 us (1%)
    pallas_call x1, Pallas kernels, on_device(): pl.pallas_call(functools.partial(kernel, n, ndp, unroll), out_shape=(jax....  57 us
    unnamed x7, local copies, waits for them, and re-layouts  2.98 us

profile of v2, /device:TPU:0, one launch (start us, length us, event | category | flops | bytes accessed | tf_op | source)
XLA Modules:
  0.0 60.6 jit_solution(6327465683646101996)
XLA Ops:
  0.6 57.0 %shard_map.76 = (bf16[8,24,512]{2,1,0:T(8,128)(2,1)}, bf16[8,24,512]{2,1,0:T(8,128)(2,1)}, f32[1,4096]{1,0:T(1,128)}) custom-call(bf16[128,4096]{1,0:T(8,128)(2,1)} %bitcast.6, bf16[128,4096]{1,0:T(8,128)(2,1)} %bitcast.7, bf16[8,24,512]{2,1,0:T(8,128)(2,1)} %bitcast.8, bf16[8,24,512]{2,1,0:T(8,128)(2,1)} %bitcast.9, f32[1,4096]{1,0:T(1,128)} %g_ref.1), custom_call_target="tpu_custom_call" | custom-call | tf_op jit(solution)/shard_map/pallas_call | solution.py:378
  57.6 0.0 copy-start
  57.6 1.7 %copy.11 = bf16[1,8,24,512]{3,2,1,0:T(8,128)(2,1)} copy(bf16[1,8,24,512]{3,2,1,0:T(8,128)(2,1)} %bitcast.11) | data formatting | bytes 393216
  59.3 0.0 copy-done
  59.3 0.0 copy-start.1
  59.3 0.7 %copy.12 = bf16[1,8,24,512]{3,2,1,0:T(8,128)(2,1)} copy(bf16[1,8,24,512]{3,2,1,0:T(8,128)(2,1)S(1)} %bitcast.10) | data formatting | bytes 393216
  60.0 0.0 copy-done.1
  60.0 0.6 copy.13
Async XLA Ops:
  57.6 1.7 %copy-start = (bf16[8,24,512]{2,1,0:T(8,128)(2,1)S(1)}, bf16[8,24,512]{2,1,0:T(8,128)(2,1)}, u32[]{:S(2)}) copy-start(bf16[8,24,512]{2,1,0:T(8,128)(2,1)} %get-tuple-element.7) | copy-start | bytes 589828
  59.3 0.7 %copy-start.1 = (f32[1,4096]{1,0:T(1,128)S(1)}, f32[1,4096]{1,0:T(1,128)}, u32[]{:S(2)}) copy-start(f32[1,4096]{1,0:T(1,128)} %get-tuple-element.14) | copy-start | bytes 49156

commit v3 on v2

--- a/solution.py
+++ b/solution.py
@@ -28,9 +28,9 @@
     x_ref, ct_ref, k_ref, v_ref, g_ref,
     kout_ref, vout_ref, gout_ref,
     xin, cin, gin, stat, kd, vd, kdt, vdt, gt, xs, qs, probs, plow, raws, ds, grads,
-    red, inv, ar, ktot, vtot, gsend, gmid, gdp,
+    red, inv, ar, ktot, vtot, gsend, gdp,
     x_send, x_recv, c_send, c_recv, g_send, g_recv, st_send, st_recv,
-    ar_send, ar_recv, gm_send, gm_recv, dp_send, dp_recv, loc,
+    ar_send, ar_recv, dp_send, dp_recv, loc,
 ):
     me = lax.axis_index("section")
     doc = lax.axis_index("dp")
@@ -47,12 +47,6 @@
             return c
         lax.fori_loop(first, last, step, 0)
 
-    def docs(body):
-        def step(j, c):
-            body(lax.rem(doc + j, ndp))
-            return c
-        lax.fori_loop(1, ndp, step, 0)
-
     def each(body, first=0, last=n, u=None):
         def step(m, c):
             body(m)
@@ -67,10 +61,12 @@
             src_ref=source, dst_ref=target, send_sem=send, recv_sem=recv,
             device_id={"section": p}, device_id_type=MESH)
 
-    def to_doc(p, source, target, send, recv):
-        return pltpu.make_async_remote_copy(
-            src_ref=source, dst_ref=target, send_sem=send, recv_sem=recv,
-            device_id={"dp": p}, device_id_type=MESH)
+    def others(body):
+        def step(j, c):
+            place = lax.rem(doc * n + me + j, n * ndp)
+            body(lax.div(place, n), lax.rem(place, n))
+            return c
+        lax.fori_loop(1, n * ndp, step, 0)
 
     def cut(ref, p):
         return ref.at[:, pl.ds(pl.multiple_of(p * cols, LANES), cols)]
@@ -94,15 +90,15 @@
     def share(a, h):
         peers(lambda p: ar_copy(a, h, p, me).start())
 
-    def gm_copy(p, slot):
-        return to(p, gsend.at[p], gmid.at[slot], gm_send.at[p], gm_recv.at[slot])
-
-    def dp_copy(p, slot):
-        return to_doc(p, gmid, gdp.at[slot], dp_send.at[p], dp_recv.at[slot])
+    def dp_copy(q, p, from_doc, slot):
+        return pltpu.make_async_remote_copy(
+            src_ref=gsend.at[p], dst_ref=gdp.at[from_doc, slot],
+            send_sem=dp_send.at[q, p], recv_sem=dp_recv.at[from_doc, slot],
+            device_id={"dp": q, "section": p}, device_id_type=MESH)
 
     barrier = pltpu.get_barrier_semaphore()
-    peers(lambda p: pl.semaphore_signal(barrier, inc=1, device_id={"section": p}, device_id_type=MESH))
-    docs(lambda p: pl.semaphore_signal(barrier, inc=1, device_id={"dp": p}, device_id_type=MESH))
+    others(lambda q, p: pl.semaphore_signal(
+        barrier, inc=1, device_id={"dp": q, "section": p}, device_id_type=MESH))
 
     total = jnp.zeros((tok, LANES), F32)
     for b in range(width // LANES):
@@ -110,7 +106,7 @@
         total = total + part * part
     stat[me] = jnp.sum(total.T, axis=0, keepdims=True)
 
-    pl.semaphore_wait(barrier, n + ndp - 2)
+    pl.semaphore_wait(barrier, n * ndp - 1)
 
     peers(lambda p: g_copy(p, me).start())
     peers(lambda p: st_copy(p, me).start())
@@ -308,14 +304,12 @@
         gsend[m] = jnp.sum(steps * k_ref[m].astype(F32), axis=0, keepdims=True) / gin[m]
 
     each(last)
-    peers(lambda p: gm_copy(p, me).start())
-    gmid[me] = gsend[me]
+    others(lambda q, p: dp_copy(q, p, doc, me).start())
+    gdp[doc, me] = gsend[me]
 
     each(lambda m: value_step(TICKS - 1, m))
     for k in range(1, TICKS - 1):
         each(lambda m: value_step(k, m))
-    peers(lambda p: gm_copy(p, p).wait_recv())
-    docs(lambda p: dp_copy(p, doc).start())
 
     def finish(m):
         value_step(0, m)
@@ -331,12 +325,10 @@
         for a in range(2 * (TICKS - 1)):
             for h in range(2):
                 ar_copy(a, h, p, me).wait_send()
-        gm_copy(p, me).wait_send()
 
     peers(drain)
-    gdp[doc] = gmid[...]
-    docs(lambda p: dp_copy(p, p).wait_recv())
-    docs(lambda p: dp_copy(p, doc).wait_send())
+    others(lambda q, p: dp_copy(q, p, q, p).wait_recv())
+    others(lambda q, p: dp_copy(q, p, doc, me).wait_send())
     for s in range(n):
         out = gdp[0, s]
         for d in range(1, ndp):
@@ -368,9 +360,9 @@
         vmem((n, 1, tok), F32), vmem((TICKS, n, 1, tok), F32),
         vmem((rounds, n, n, 1, tok), F32),
         vmem((n, src, cols), F32), vmem((n, src, cols), F32),
-        vmem((n, 1, cols), F32), vmem((n, 1, cols), F32), vmem((ndp, n, 1, cols), F32),
+        vmem((n, 1, cols), F32), vmem((ndp, n, 1, cols), F32),
         sem((n,)), sem((n,)), sem((n,)), sem((n,)), sem((n,)), sem((n,)), sem((n,)), sem((n,)),
-        sem((rounds, 2, n)), sem((rounds, 2, n)), sem((n,)), sem((n,)), sem((ndp,)), sem((ndp,)), sem((3,)),
+        sem((rounds, 2, n)), sem((rounds, 2, n)), sem((ndp, n)), sem((ndp, n)), sem((3,)),
     ]
     in_vmem = pl.BlockSpec(memory_space=pltpu.VMEM)
     in_place = pl.BlockSpec(memory_space=pl.ANY)

time: 60.9 us -> 59.8 us (0.982)
  Pallas kernels: 57 us -> 55.9 us
    pallas_call x1, Pallas kernels: 57 us -> 55.9 us  [on_device(): pl.pallas_call(functools.partial(kernel, n, ndp, unroll), out_shape=(jax....]
where the time goes in v3:
time: 59.8 us; the launch traced here: 59.5 us
  Pallas kernels  55.9 us (93%)
  local copies, waits for them, and re-layouts  2.98 us (5%)
  between operations  0.65 us (1%)
    pallas_call x1, Pallas kernels, on_device(): pl.pallas_call(functools.partial(kernel, n, ndp, unroll), out_shape=(jax....  55.9 us
    unnamed x7, local copies, waits for them, and re-layouts  2.98 us

profile of v3, /device:TPU:0, one launch (start us, length us, event | category | flops | bytes accessed | tf_op | source)
XLA Modules:
  0.0 59.5 jit_solution(17536774270067663544)
XLA Ops:
  0.6 55.9 %shard_map.76 = (bf16[8,24,512]{2,1,0:T(8,128)(2,1)}, bf16[8,24,512]{2,1,0:T(8,128)(2,1)}, f32[1,4096]{1,0:T(1,128)}) custom-call(bf16[128,4096]{1,0:T(8,128)(2,1)} %bitcast.6, bf16[128,4096]{1,0:T(8,128)(2,1)} %bitcast.7, bf16[8,24,512]{2,1,0:T(8,128)(2,1)} %bitcast.8, bf16[8,24,512]{2,1,0:T(8,128)(2,1)} %bitcast.9, f32[1,4096]{1,0:T(1,128)} %g_ref.1), custom_call_target="tpu_custom_call" | custom-call | tf_op jit(solution)/shard_map/pallas_call | solution.py:370
  56.5 0.0 copy-start
  56.6 1.7 %copy.11 = bf16[1,8,24,512]{3,2,1,0:T(8,128)(2,1)} copy(bf16[1,8,24,512]{3,2,1,0:T(8,128)(2,1)} %bitcast.11) | data formatting | bytes 393216
  58.2 0.0 copy-done
  58.2 0.0 copy-start.1
  58.2 0.7 %copy.12 = bf16[1,8,24,512]{3,2,1,0:T(8,128)(2,1)} copy(bf16[1,8,24,512]{3,2,1,0:T(8,128)(2,1)S(1)} %bitcast.10) | data formatting | bytes 393216
  58.9 0.0 copy-done.1
  58.9 0.6 %copy.13 = f32[1,4096]{1,0:T(1,128)} copy(f32[1,4096]{1,0:T(1,128)S(1)} %copy-done.1) | data formatting | bytes 32768
Async XLA Ops:
  56.5 1.7 %copy-start = (bf16[8,24,512]{2,1,0:T(8,128)(2,1)S(1)}, bf16[8,24,512]{2,1,0:T(8,128)(2,1)}, u32[]{:S(2)}) copy-start(bf16[8,24,512]{2,1,0:T(8,128)(2,1)} %get-tuple-element.7) | copy-start | bytes 589828
  58.2 0.7 %copy-start.1 = (f32[1,4096]{1,0:T(1,128)S(1)}, f32[1,4096]{1,0:T(1,128)}, u32[]{:S(2)}) copy-start(f32[1,4096]{1,0:T(1,128)} %get-tuple-element.14) | copy-start | bytes 49156
